TPU v7x, 256 devices: a whole 4x4x8 slice. The times are simulated.
256 devices in a mesh: frames: 8 (over x, core), rows: 32 (over y, z).
Axes of the slice: x: 4, y: 4, z: 8, core: 2. Of those that a mesh axis runs over, the one named last changes fastest.
Arguments:
- observed: float32 [32, 2048, 2048], P('frames', 'rows'), may hold values from 0.25 to 4
- kernel: float32 [2048, 65], P('rows'), may hold values from 0.004 to 0.04
- row_shift: int32 [2048], P('rows'), may hold values from -8 to 8
- cycle_map: float32 [2048, 256], P('rows'), may hold values from 0 to 0.03125
- cycle_blocks: int32 [32, 8], P('rows'), may hold values from 0 to 63
- chi_map: bfloat16 [32, 2048, 720], P('rows'), may hold values from 0 to 3.0517578e-05
Outputs:
- binned: float32 [2048, 720], P('rows')
All inputs are finite; a program needn't handle non-finite values.
Results may differ from a plain program's by a relative error of at most 0.0003.
Values sent between devices are 32-bit elements; how exact they have to be, the bound alone decides.
A program may use at most 128 MiB of HBM per device.

v0:
```python
import jax
import jax.numpy as jnp
from jax import lax
from jax.sharding import PartitionSpec as P

SHIFT = 8
ITERS = 4
Q = 2048
CHI = 720
QB = 32
NB = 8


def shifted(block, axis, distance):
    devices = range(lax.axis_size(axis))
    route = [(i - distance, i) for i in devices if i - distance in devices]
    return lax.ppermute(block, axis, route)


def extended(cells, sides, width):
    for axis, dim in sides:
        count = lax.axis_size(axis)
        ends = count - 1
        head = lax.slice_in_dim(cells, 0, width, axis=dim)
        tail = lax.slice_in_dim(cells, cells.shape[dim] - width, cells.shape[dim], axis=dim)
        cells = jnp.concatenate(
            [
                lax.ppermute(tail, axis, [(i, (i + 1) % count) for i in range(ends)]),
                cells,
                lax.ppermute(head, axis, [((i + 1) % count, i) for i in range(ends)]),
            ],
            axis=dim,
        )
    return cells


def band_matrix(kernel, row_shift, first_row, total_rows, halo_rows):
    rows_here = kernel.shape[0]
    band_width = kernel.shape[1]
    half_band = (band_width - 1) // 2
    local_rows = jnp.arange(rows_here, dtype=jnp.int32)[:, None]
    tap_index = jnp.arange(band_width, dtype=jnp.int32)[None, :]
    target = local_rows + row_shift[:, None] + tap_index - half_band
    global_rows = target + first_row
    inside = (global_rows >= 0) & (global_rows < total_rows)
    weights = jnp.where(inside, kernel, jnp.float32(0.0))
    columns = jnp.arange(rows_here + 2 * halo_rows, dtype=jnp.int32)
    matches = (target[:, :, None] + halo_rows == columns[None, None, :]).astype(jnp.float32)
    return jnp.einsum("ik,ikj->ij", weights, matches, precision=lax.Precision.HIGHEST)


def rim_tables(rows_here, halo_rows):
    top_place = jnp.eye(halo_rows, rows_here, dtype=jnp.float32)
    bottom_place = jnp.eye(halo_rows, rows_here, k=rows_here - halo_rows, dtype=jnp.float32)
    return (top_place, bottom_place)


def body(observed, kernel, row_shift, cycle_map, cycle_blocks, chi_map):
    rows_here = observed.shape[1]
    tile_count = lax.axis_size("rows")
    first_row = lax.axis_index("rows") * rows_here
    halo_rows = (kernel.shape[1] - 1) // 2 + SHIFT
    band_mat = band_matrix(kernel, row_shift, first_row, rows_here * tile_count, halo_rows)
    top_place, bottom_place = rim_tables(rows_here, halo_rows)
    upper_band = band_mat[:, :halo_rows]
    centre_band = band_mat[:, halo_rows : halo_rows + rows_here]
    lower_band = band_mat[:, halo_rows + rows_here :]

    def spread(upper_rim, centre, lower_rim):
        from_below = shifted(upper_rim, "rows", -1)
        from_above = shifted(lower_rim, "rows", 1)
        centre = centre + jnp.einsum(
            "hr,fhc->frc", top_place, from_above, precision=lax.Precision.HIGHEST
        )
        return centre + jnp.einsum(
            "hr,fhc->frc", bottom_place, from_below, precision=lax.Precision.HIGHEST
        )

    norm_sums = spread(
        jnp.sum(upper_band, axis=0)[None, :, None],
        jnp.sum(centre_band, axis=0)[None, :, None],
        jnp.sum(lower_band, axis=0)[None, :, None],
    )
    estimate = observed
    for repeat in range(ITERS):
        padded = extended(estimate, (("rows", 1),), halo_rows)
        blurred = jnp.einsum("ij,fjc->fic", band_mat, padded, precision=lax.Precision.HIGHEST)
        ratios = observed / blurred
        upper_part = jnp.einsum("ij,fic->fjc", upper_band, ratios, precision=lax.Precision.HIGHEST)
        centre_part = jnp.einsum(
            "ij,fic->fjc", centre_band, ratios, precision=lax.Precision.HIGHEST
        )
        lower_part = jnp.einsum("ij,fic->fjc", lower_band, ratios, precision=lax.Precision.HIGHEST)
        backed = spread(upper_part, centre_part, lower_part)
        estimate = estimate * backed / norm_sums
    summed = jnp.sum(estimate, axis=0)
    cycle_part = jnp.einsum("rq,rc->qc", cycle_map, summed, precision=lax.Precision.HIGHEST).astype(
        jnp.bfloat16
    )
    blocks = jnp.dot(cycle_part, chi_map[0], preferred_element_type=jnp.float32).reshape(
        NB, QB, CHI
    )
    onehot = (jnp.arange(Q // QB, dtype=jnp.int32)[:, None] == cycle_blocks[0][None, :]).astype(
        jnp.float32
    )
    owned = lax.psum_scatter(
        jnp.einsum("kb,bqc->kqc", onehot, blocks, precision=lax.Precision.HIGHEST).reshape(Q, CHI),
        "rows",
        scatter_dimension=0,
        tiled=True,
    )
    binned = lax.psum(owned, "frames")
    return binned


def solution(mesh):
    return jax.shard_map(
        body,
        mesh=mesh,
        in_specs=(
            P("frames", "rows", None),
            P("rows", None),
            P("rows"),
            P("rows", None),
            P("rows", None),
            P("rows", None, None),
        ),
        out_specs=P("rows", None),
        check_vma=False,
    )
```

profile of v0, /device:TPU:8, one launch (start us, length us, event | category | flops | bytes accessed | tf_op | source)
XLA Modules:
  0.0 628.5 jit_solution(18317069830610186839)
XLA Ops:
  6.5 3.7 fusion.137
  10.2 3.8 collective-permute-start
  14.0 5.7 collective-permute-start.1
  22.3 24.7 %collective-permute-done = f32[4,40,2048]{2,1,0:T(8,128)} collective-permute-done((f32[4,40,2048]{2,1,0:T(8,128)}, f32[4,40,2048]{2,1,0:T(8,128)}, u32[]{:S(2)}, u32[]{:S(2)}) %collective-permute-start) | collective-permute-done | bytes 1310752 | tf_op jit(solution)/shard_map/ppermute | solution.py:28
  48.1 6.2 fusion.52
  59.8 6.0 collective-permute-start.3
  66.0 3.9 collective-permute-start.5
  72.1 20.9 %collective-permute-done.5 = f32[1,40,1]{1,2,0:T(1,128)S(1)} collective-permute-done((f32[1,40,1]{1,2,0:T(1,128)S(1)}, f32[1,40,1]{1,2,0:T(1,128)S(1)}, u32[]{:S(2)}, u32[]{:S(2)}) %collective-permute-start.5) | collective-permute-done | bytes 192 | tf_op jit(solution)/shard_map/ppermute | solution.py:17
  99.1 4.0 collective-permute-start.6
  103.1 4.4 collective-permute-start.7
  107.5 25.0 %collective-permute-done.6 = f32[4,40,2048]{2,1,0:T(8,128)S(1)} collective-permute-done((f32[4,40,2048]{2,1,0:T(8,128)S(1)}, f32[4,40,2048]{2,1,0:T(8,128)S(1)}, u32[]{:S(2)}, u32[]{:S(2)}) %collective-permute-start.6) | collective-permute-done | bytes 1310752 | tf_op jit(solution)/shard_map/ppermute | solution.py:28
  142.7 5.9 collective-permute-start.9
  150.7 20.2 %collective-permute-done.8 = f32[4,40,2048]{2,1,0:T(8,128)S(1)} collective-permute-done((f32[4,40,2048]{2,1,0:T(8,128)S(1)}, f32[4,40,2048]{2,1,0:T(8,128)S(1)}, u32[]{:S(2)}, u32[]{:S(2)}) %collective-permute-start.8) | collective-permute-done | bytes 1310752 | tf_op jit(solution)/shard_map/ppermute | solution.py:17
  177.5 6.5 %collective-permute-start.11 = (f32[4,40,2048]{2,1,0:T(8,128)S(1)}, f32[4,40,2048]{2,1,0:T(8,128)S(1)}, u32[]{:S(2)}, u32[]{:S(2)}) collective-permute-start(f32[4,40,2048]{2,1,0:T(8,128)S(1)} %get-tuple-element.10), channel_id=1, source_target_pairs={{1,0},{2,1},{3,2},{4,3},{5,4},{6,5},{7,6},{8,7},{9,8},{10,9},{11,1... | collective-permute-start | bytes 3932168 | tf_op jit(solution)/shard_map/ppermute | solution.py:30
  184.0 23.1 %collective-permute-done.10 = f32[4,40,2048]{2,1,0:T(8,128)S(1)} collective-permute-done((f32[4,40,2048]{2,1,0:T(8,128)S(1)}, f32[4,40,2048]{2,1,0:T(8,128)S(1)}, u32[]{:S(2)}, u32[]{:S(2)}) %collective-permute-start.10) | collective-permute-done | bytes 1310752 | tf_op jit(solution)/shard_map/ppermute | solution.py:28
  216.5 7.0 %collective-permute-start.13 = (f32[4,40,2048]{2,1,0:T(8,128)S(1)}, f32[4,40,2048]{2,1,0:T(8,128)S(1)}, u32[]{:S(2)}, u32[]{:S(2)}) collective-permute-start(f32[4,40,2048]{2,1,0:T(8,128)S(1)} %convolution_bitcast_fusion.2), channel_id=1, source_target_pairs={{1,0},{2,1},{3,2},{4,3},{5,4},{6,5},{7,6},{8,7},{9,8},{10,9},{11,1... | collective-permute-start | bytes 3932168 | tf_op jit(solution)/shard_map/ppermute | solution.py:17
  225.5 18.1 %collective-permute-done.12 = f32[4,40,2048]{2,1,0:T(8,128)S(1)} collective-permute-done((f32[4,40,2048]{2,1,0:T(8,128)S(1)}, f32[4,40,2048]{2,1,0:T(8,128)S(1)}, u32[]{:S(2)}, u32[]{:S(2)}) %collective-permute-start.12) | collective-permute-done | bytes 1310752 | tf_op jit(solution)/shard_map/ppermute | solution.py:17
  250.3 6.5 %collective-permute-start.15 = (f32[4,40,2048]{2,1,0:T(8,128)S(1)}, f32[4,40,2048]{2,1,0:T(8,128)S(1)}, u32[]{:S(2)}, u32[]{:S(2)}) collective-permute-start(f32[4,40,2048]{2,1,0:T(8,128)S(1)} %get-tuple-element.8), channel_id=1, source_target_pairs={{1,0},{2,1},{3,2},{4,3},{5,4},{6,5},{7,6},{8,7},{9,8},{10,9},{11,1... | collective-permute-start | bytes 3932168 | tf_op jit(solution)/shard_map/ppermute | solution.py:30
  256.9 21.3 %collective-permute-done.14 = f32[4,40,2048]{2,1,0:T(8,128)S(1)} collective-permute-done((f32[4,40,2048]{2,1,0:T(8,128)S(1)}, f32[4,40,2048]{2,1,0:T(8,128)S(1)}, u32[]{:S(2)}, u32[]{:S(2)}) %collective-permute-start.14) | collective-permute-done | bytes 1310752 | tf_op jit(solution)/shard_map/ppermute | solution.py:28
  287.5 6.7 %collective-permute-start.17 = (f32[4,40,2048]{2,1,0:T(8,128)S(1)}, f32[4,40,2048]{2,1,0:T(8,128)S(1)}, u32[]{:S(2)}, u32[]{:S(2)}) collective-permute-start(f32[4,40,2048]{2,1,0:T(8,128)S(1)} %convolution_bitcast_fusion), channel_id=1, source_target_pairs={{1,0},{2,1},{3,2},{4,3},{5,4},{6,5},{7,6},{8,7},{9,8},{10,9},{11,1... | collective-permute-start | bytes 3932168 | tf_op jit(solution)/shard_map/ppermute | solution.py:17
  296.2 16.5 %collective-permute-done.16 = f32[4,40,2048]{2,1,0:T(8,128)S(1)} collective-permute-done((f32[4,40,2048]{2,1,0:T(8,128)S(1)}, f32[4,40,2048]{2,1,0:T(8,128)S(1)}, u32[]{:S(2)}, u32[]{:S(2)}) %collective-permute-start.16) | collective-permute-done | bytes 1310752 | tf_op jit(solution)/shard_map/ppermute | solution.py:17
  322.8 6.3 %copy.21 = f32[64,32,720]{2,1,0:T(8,128)} copy(f32[64,32,720]{2,0,1:T(8,128)S(1)} %fusion.67) | data formatting | bytes 11796480 | tf_op jit(solution)/shard_map/kb,bqc->kqc/dot_general | solution.py:107
  329.2 224.2 %reduce-scatter.2.cloned.1.call-done = f32[64,720]{1,0:T(8,128)} async-done(((f32[2048,720]{1,0:T(8,128)}), f32[64,720]{1,0:T(8,128)}) %reduce-scatter.2.cloned.1.call-update) | async-done | bytes 184336 | tf_op jit(solution)/shard_map/reduce_scatter | solution.py:106
  553.5 66.4 %all-reduce.2.cloned.1.call-done = f32[64,720]{1,0:T(8,128)} async-done(((f32[64,720]{1,0:T(8,128)}), f32[64,720]{1,0:T(8,128)}) %all-reduce.2.cloned.1.call-update) | async-done | bytes 184336 | tf_op jit(solution)/shard_map/psum | solution.py:112
  (73 shorter events, 77.3 us)
Async XLA Ops:
  6.5 312.5 %copy-start = (bf16[1,2048,720]{1,2,0:T(8,128)(2,1)S(1)}, bf16[1,2048,720]{1,2,0:T(8,128)(2,1)}, u32[]{:S(2)}) copy-start(bf16[1,2048,720]{1,2,0:T(8,128)(2,1)} %param.11) | copy-start | bytes 8847364
  6.5 13.3 %copy-start.5 = (s32[64]{0:T(128)S(1)}, s32[64]{0:T(128)}, u32[]{:S(2)}) copy-start(s32[64]{0:T(128)} %param.8) | copy-start | bytes 772
  6.5 13.4 %copy-start.3 = (f32[64,65]{1,0:T(8,128)S(1)}, f32[64,65]{1,0:T(8,128)}, u32[]{:S(2)}) copy-start(f32[64,65]{1,0:T(8,128)} %param.7) | copy-start | bytes 49924
  6.5 546.9 %reduce-scatter.2.cloned.1.call-start = ((), (), s32[]{:S(2)}) async-start(), calls=%async_computation.1 | async-start | bytes 6488064 | tf_op jit(solution)/shard_map/reduce_scatter | solution.py:106
  10.2 36.7 %collective-permute-start = (f32[4,40,2048]{2,1,0:T(8,128)}, f32[4,40,2048]{2,1,0:T(8,128)}, u32[]{:S(2)}, u32[]{:S(2)}) collective-permute-start(f32[4,40,2048]{2,1,0:T(8,128)} %get-tuple-element.13), channel_id=1, source_target_pairs={{0,1},{1,2},{2,3},{3,4},{4,5},{5,6},{6,7},{7,8},{8,9},{9,10},{10,1... | collective-permute-start | bytes 3932168 | tf_op jit(solution)/shard_map/ppermute | solution.py:28
  14.0 34.1 %collective-permute-start.1 = (f32[4,40,2048]{2,1,0:T(8,128)}, f32[4,40,2048]{2,1,0:T(8,128)}, u32[]{:S(2)}, u32[]{:S(2)}) collective-permute-start(f32[4,40,2048]{2,1,0:T(8,128)} %get-tuple-element.14), channel_id=1, source_target_pairs={{1,0},{2,1},{3,2},{4,3},{5,4},{6,5},{7,6},{8,7},{9,8},{10,9},{11,1... | collective-permute-start | bytes 3932168 | tf_op jit(solution)/shard_map/ppermute | solution.py:30
  55.9 39.6 %collective-permute-start.2 = (f32[4,40,2048]{2,1,0:T(8,128)S(1)}, f32[4,40,2048]{2,1,0:T(8,128)S(1)}, u32[]{:S(2)}, u32[]{:S(2)}) collective-permute-start(f32[4,40,2048]{2,1,0:T(8,128)S(1)} %convolution_bitcast_fusion.7), channel_id=1, source_target_pairs={{0,1},{1,2},{2,3},{3,4},{4,5},{5,6},{6,7},{7,8},{8,9},{9,10},{10,1... | collective-permute-start | bytes 3932168 | tf_op jit(solution)/shard_map/ppermute | solution.py:17
  59.8 37.0 %collective-permute-start.3 = (f32[4,40,2048]{2,1,0:T(8,128)S(1)}, f32[4,40,2048]{2,1,0:T(8,128)S(1)}, u32[]{:S(2)}, u32[]{:S(2)}) collective-permute-start(f32[4,40,2048]{2,1,0:T(8,128)S(1)} %convolution_bitcast_fusion.6), channel_id=1, source_target_pairs={{1,0},{2,1},{3,2},{4,3},{5,4},{6,5},{7,6},{8,7},{9,8},{10,9},{11,1... | collective-permute-start | bytes 3932168 | tf_op jit(solution)/shard_map/ppermute | solution.py:17
  66.0 27.1 %collective-permute-start.5 = (f32[1,40,1]{1,2,0:T(1,128)S(1)}, f32[1,40,1]{1,2,0:T(1,128)S(1)}, u32[]{:S(2)}, u32[]{:S(2)}) collective-permute-start(f32[1,40,1]{1,2,0:T(1,128)S(1)} %bitcast.192), channel_id=1, source_target_pairs={{1,0},{2,1},{3,2},{4,3},{5,4},{6,5},{7,6},{8,7},{9,8},{10,9},{11,1... | collective-permute-start | bytes 488 | tf_op jit(solution)/shard_map/ppermute | solution.py:17
  69.9 23.3 %collective-permute-start.4 = (f32[1,40,1]{1,2,0:T(1,128)S(1)}, f32[1,40,1]{1,2,0:T(1,128)S(1)}, u32[]{:S(2)}, u32[]{:S(2)}) collective-permute-start(f32[1,40,1]{1,2,0:T(1,128)S(1)} %bitcast.191), channel_id=1, source_target_pairs={{0,1},{1,2},{2,3},{3,4},{4,5},{5,6},{6,7},{7,8},{8,9},{9,10},{10,1... | collective-permute-start | bytes 488 | tf_op jit(solution)/shard_map/ppermute | solution.py:17
  99.1 33.4 %collective-permute-start.6 = (f32[4,40,2048]{2,1,0:T(8,128)S(1)}, f32[4,40,2048]{2,1,0:T(8,128)S(1)}, u32[]{:S(2)}, u32[]{:S(2)}) collective-permute-start(f32[4,40,2048]{2,1,0:T(8,128)S(1)} %get-tuple-element.11), channel_id=1, source_target_pairs={{0,1},{1,2},{2,3},{3,4},{4,5},{5,6},{6,7},{7,8},{8,9},{9,10},{10,1... | collective-permute-start | bytes 3932168 | tf_op jit(solution)/shard_map/ppermute | solution.py:28
  103.1 30.6 %collective-permute-start.7 = (f32[4,40,2048]{2,1,0:T(8,128)S(1)}, f32[4,40,2048]{2,1,0:T(8,128)S(1)}, u32[]{:S(2)}, u32[]{:S(2)}) collective-permute-start(f32[4,40,2048]{2,1,0:T(8,128)S(1)} %get-tuple-element.12), channel_id=1, source_target_pairs={{1,0},{2,1},{3,2},{4,3},{5,4},{6,5},{7,6},{8,7},{9,8},{10,9},{11,1... | collective-permute-start | bytes 3932168 | tf_op jit(solution)/shard_map/ppermute | solution.py:30
  138.4 32.5 %collective-permute-start.8 = (f32[4,40,2048]{2,1,0:T(8,128)S(1)}, f32[4,40,2048]{2,1,0:T(8,128)S(1)}, u32[]{:S(2)}, u32[]{:S(2)}) collective-permute-start(f32[4,40,2048]{2,1,0:T(8,128)S(1)} %convolution_bitcast_fusion.5), channel_id=1, source_target_pairs={{0,1},{1,2},{2,3},{3,4},{4,5},{5,6},{6,7},{7,8},{8,9},{9,10},{10,1... | collective-permute-start | bytes 3932168 | tf_op jit(solution)/shard_map/ppermute | solution.py:17
  142.7 30.9 %collective-permute-start.9 = (f32[4,40,2048]{2,1,0:T(8,128)S(1)}, f32[4,40,2048]{2,1,0:T(8,128)S(1)}, u32[]{:S(2)}, u32[]{:S(2)}) collective-permute-start(f32[4,40,2048]{2,1,0:T(8,128)S(1)} %convolution_bitcast_fusion.4), channel_id=1, source_target_pairs={{1,0},{2,1},{3,2},{4,3},{5,4},{6,5},{7,6},{8,7},{9,8},{10,9},{11,1... | collective-permute-start | bytes 3932168 | tf_op jit(solution)/shard_map/ppermute | solution.py:17
  175.6 31.6 %collective-permute-start.10 = (f32[4,40,2048]{2,1,0:T(8,128)S(1)}, f32[4,40,2048]{2,1,0:T(8,128)S(1)}, u32[]{:S(2)}, u32[]{:S(2)}) collective-permute-start(f32[4,40,2048]{2,1,0:T(8,128)S(1)} %get-tuple-element.9), channel_id=1, source_target_pairs={{0,1},{1,2},{2,3},{3,4},{4,5},{5,6},{6,7},{7,8},{8,9},{9,10},{10,1... | collective-permute-start | bytes 3932168 | tf_op jit(solution)/shard_map/ppermute | solution.py:28
  177.5 30.8 %collective-permute-start.11 = (f32[4,40,2048]{2,1,0:T(8,128)S(1)}, f32[4,40,2048]{2,1,0:T(8,128)S(1)}, u32[]{:S(2)}, u32[]{:S(2)}) collective-permute-start(f32[4,40,2048]{2,1,0:T(8,128)S(1)} %get-tuple-element.10), channel_id=1, source_target_pairs={{1,0},{2,1},{3,2},{4,3},{5,4},{6,5},{7,6},{8,7},{9,8},{10,9},{11,1... | collective-permute-start | bytes 3932168 | tf_op jit(solution)/shard_map/ppermute | solution.py:30
  213.0 30.6 %collective-permute-start.12 = (f32[4,40,2048]{2,1,0:T(8,128)S(1)}, f32[4,40,2048]{2,1,0:T(8,128)S(1)}, u32[]{:S(2)}, u32[]{:S(2)}) collective-permute-start(f32[4,40,2048]{2,1,0:T(8,128)S(1)} %convolution_bitcast_fusion.3), channel_id=1, source_target_pairs={{0,1},{1,2},{2,3},{3,4},{4,5},{5,6},{6,7},{7,8},{8,9},{9,10},{10,1... | collective-permute-start | bytes 3932168 | tf_op jit(solution)/shard_map/ppermute | solution.py:17
  216.5 29.9 %collective-permute-start.13 = (f32[4,40,2048]{2,1,0:T(8,128)S(1)}, f32[4,40,2048]{2,1,0:T(8,128)S(1)}, u32[]{:S(2)}, u32[]{:S(2)}) collective-permute-start(f32[4,40,2048]{2,1,0:T(8,128)S(1)} %convolution_bitcast_fusion.2), channel_id=1, source_target_pairs={{1,0},{2,1},{3,2},{4,3},{5,4},{6,5},{7,6},{8,7},{9,8},{10,9},{11,1... | collective-permute-start | bytes 3932168 | tf_op jit(solution)/shard_map/ppermute | solution.py:17
  248.4 29.7 %collective-permute-start.14 = (f32[4,40,2048]{2,1,0:T(8,128)S(1)}, f32[4,40,2048]{2,1,0:T(8,128)S(1)}, u32[]{:S(2)}, u32[]{:S(2)}) collective-permute-start(f32[4,40,2048]{2,1,0:T(8,128)S(1)} %get-tuple-element.7), channel_id=1, source_target_pairs={{0,1},{1,2},{2,3},{3,4},{4,5},{5,6},{6,7},{7,8},{8,9},{9,10},{10,1... | collective-permute-start | bytes 3932168 | tf_op jit(solution)/shard_map/ppermute | solution.py:28
  250.3 29.0 %collective-permute-start.15 = (f32[4,40,2048]{2,1,0:T(8,128)S(1)}, f32[4,40,2048]{2,1,0:T(8,128)S(1)}, u32[]{:S(2)}, u32[]{:S(2)}) collective-permute-start(f32[4,40,2048]{2,1,0:T(8,128)S(1)} %get-tuple-element.8), channel_id=1, source_target_pairs={{1,0},{2,1},{3,2},{4,3},{5,4},{6,5},{7,6},{8,7},{9,8},{10,9},{11,1... | collective-permute-start | bytes 3932168 | tf_op jit(solution)/shard_map/ppermute | solution.py:30
  284.0 28.8 %collective-permute-start.16 = (f32[4,40,2048]{2,1,0:T(8,128)S(1)}, f32[4,40,2048]{2,1,0:T(8,128)S(1)}, u32[]{:S(2)}, u32[]{:S(2)}) collective-permute-start(f32[4,40,2048]{2,1,0:T(8,128)S(1)} %convolution_bitcast_fusion.1), channel_id=1, source_target_pairs={{0,1},{1,2},{2,3},{3,4},{4,5},{5,6},{6,7},{7,8},{8,9},{9,10},{10,1... | collective-permute-start | bytes 3932168 | tf_op jit(solution)/shard_map/ppermute | solution.py:17
  287.5 28.0 %collective-permute-start.17 = (f32[4,40,2048]{2,1,0:T(8,128)S(1)}, f32[4,40,2048]{2,1,0:T(8,128)S(1)}, u32[]{:S(2)}, u32[]{:S(2)}) collective-permute-start(f32[4,40,2048]{2,1,0:T(8,128)S(1)} %convolution_bitcast_fusion), channel_id=1, source_target_pairs={{1,0},{2,1},{3,2},{4,3},{5,4},{6,5},{7,6},{8,7},{9,8},{10,9},{11,1... | collective-permute-start | bytes 3932168 | tf_op jit(solution)/shard_map/ppermute | solution.py:17
  314.1 3.1 copy-start.2
  329.2 290.7 %all-reduce.2.cloned.1.call-start = ((), (), s32[]{:S(2)}) async-start(), calls=%async_computation.2 | async-start | bytes 393216 | tf_op jit(solution)/shard_map/psum | solution.py:112
  (2 other events, 2.6 us)
Sparse Core Ops, SparseCore 0:
  329.3 224.1 reduce-scatter.1
  555.9 63.9 all-reduce.1
where the time goes:
time: 635 us; the launch traced here: 628 us
  waiting for transfers between devices  470 us (74%)
  starting transfers between devices  75.4 us (12%)
  matrix products  56.2 us (9%)
  between operations  14.1 us (2%)
  local copies, waits for them, and re-layouts  12.8 us (2%)
    reduce_scatter x1, waiting for transfers between devices, body(): lax.psum_scatter(jnp.einsum('kb,bqc->kqc', onehot, blocks, precision=lax....  224 us
    ppermute x4, waiting for transfers between devices, extended(): lax.ppermute(tail, axis, [(i, (i + 1) % count) for i in range(ends)])  94.1 us
    ppermute x10, waiting for transfers between devices, shifted(): return lax.ppermute(block, axis, route)  80.2 us
    psum x1, waiting for transfers between devices, body(): binned = lax.psum(owned, 'frames')  66.4 us
    ppermute x10, starting transfers between devices, shifted(): return lax.ppermute(block, axis, route)  40.5 us
    ppermute x4, starting transfers between devices, extended(): lax.ppermute(head, axis, [((i + 1) % count, i) for i in range(ends)])  23.2 us
    dot_general x4, matrix products, body(): jnp.einsum('ij,fjc->fic', band_mat, padded, precision=lax.Precision.HIGHEST)  15.4 us
  transfers between devices with their start and end apart: 20, of which 17 were waited for; matrix products, arithmetic and copies ran while one was open for 4% of the time, Pallas kernels for 0%

commit v1 on v0

--- a/solution.py
+++ b/solution.py
@@ -109,7 +109,8 @@
         scatter_dimension=0,
         tiled=True,
     )
-    binned = lax.psum(owned, "frames")
+    pieces = lax.all_gather(owned, "frames", axis=0, tiled=False)
+    binned = pieces.sum(axis=0)
     return binned
 
 

time: 635 us -> 598 us (0.942)
  waiting for transfers between devices: 470 us -> 431 us
    psum x1 -> x0, waiting for transfers between devices: 66.4 us -> none  [body(): binned = lax.psum(owned, 'frames')]
    all_gather x0 -> x1, waiting for transfers between devices: none -> 28.1 us  [body(): pieces = lax.all_gather(owned, 'frames', axis=0, tiled=False)]
where the time goes in v1:
time: 598 us; the launch traced here: 591 us
  waiting for transfers between devices  431 us (72%)
  starting transfers between devices  75.4 us (13%)
  matrix products  56.1 us (9%)
  between operations  14.1 us (2%)
  local copies, waits for them, and re-layouts  11.2 us (2%)
    reduce_scatter x1, waiting for transfers between devices, body(): lax.psum_scatter(jnp.einsum('kb,bqc->kqc', onehot, blocks, precision=lax....  224 us
    ppermute x4, waiting for transfers between devices, extended(): lax.ppermute(tail, axis, [(i, (i + 1) % count) for i in range(ends)])  94.1 us
    ppermute x10, waiting for transfers between devices, shifted(): return lax.ppermute(block, axis, route)  80.2 us
    ppermute x10, starting transfers between devices, shifted(): return lax.ppermute(block, axis, route)  40.5 us
    all_gather x1, waiting for transfers between devices, body(): pieces = lax.all_gather(owned, 'frames', axis=0, tiled=False)  28.1 us
    ppermute x4, starting transfers between devices, extended(): lax.ppermute(head, axis, [((i + 1) % count, i) for i in range(ends)])  23.2 us
    dot_general x4, matrix products, body(): jnp.einsum('ij,fjc->fic', band_mat, padded, precision=lax.Precision.HIGHEST)  15.4 us
  transfers between devices with their start and end apart: 20, of which 17 were waited for; matrix products, arithmetic and copies ran while one was open for 4% of the time, Pallas kernels for 0%

profile of v1, /device:TPU:8, one launch (start us, length us, event | category | flops | bytes accessed | tf_op | source)
XLA Modules:
  0.0 590.8 jit_solution(14735502097046653515)
XLA Ops:
  6.5 3.7 fusion.137
  10.2 3.8 collective-permute-start
  14.0 5.7 collective-permute-start.1
  22.3 24.7 %collective-permute-done = f32[4,40,2048]{2,1,0:T(8,128)} collective-permute-done((f32[4,40,2048]{2,1,0:T(8,128)}, f32[4,40,2048]{2,1,0:T(8,128)}, u32[]{:S(2)}, u32[]{:S(2)}) %collective-permute-start) | collective-permute-done | bytes 1310752 | tf_op jit(solution)/shard_map/ppermute | solution.py:28
  48.1 6.2 %fusion.52 = f32[4,64,2048]{2,1,0:T(8,128)S(1)} fusion(f32[4,64,2048]{2,1,0:T(8,128)} %param.6, f32[4,40,2048]{2,1,0:T(8,128)} %collective-permute-done.1, f32[4,40,2048]{2,1,0:T(8,128)} %collective-permute-done, f32[64,1,144]{2,1,0:T(1,128)S(1)} %fusion.24), kind=kOutput, calls=%fused_computation.62 | convolution fusion | flops 908853248 | bytes 6852608 | tf_op jit(solution)/shard_map/ij,fjc->fic/dot_general | solution.py:87
  59.8 6.0 %collective-permute-start.3 = (f32[4,40,2048]{2,1,0:T(8,128)S(1)}, f32[4,40,2048]{2,1,0:T(8,128)S(1)}, u32[]{:S(2)}, u32[]{:S(2)}) collective-permute-start(f32[4,40,2048]{2,1,0:T(8,128)S(1)} %convolution_bitcast_fusion.6), channel_id=1, source_target_pairs={{1,0},{2,1},{3,2},{4,3},{5,4},{6,5},{7,6},{8,7},{9,8},{10,9},{11,1... | collective-permute-start | bytes 3932168 | tf_op jit(solution)/shard_map/ppermute | solution.py:17
  66.0 3.9 collective-permute-start.5
  72.1 20.9 %collective-permute-done.5 = f32[1,40,1]{1,2,0:T(1,128)S(1)} collective-permute-done((f32[1,40,1]{1,2,0:T(1,128)S(1)}, f32[1,40,1]{1,2,0:T(1,128)S(1)}, u32[]{:S(2)}, u32[]{:S(2)}) %collective-permute-start.5) | collective-permute-done | bytes 192 | tf_op jit(solution)/shard_map/ppermute | solution.py:17
  99.1 4.0 collective-permute-start.6
  103.1 4.4 collective-permute-start.7
  107.5 25.0 %collective-permute-done.6 = f32[4,40,2048]{2,1,0:T(8,128)S(1)} collective-permute-done((f32[4,40,2048]{2,1,0:T(8,128)S(1)}, f32[4,40,2048]{2,1,0:T(8,128)S(1)}, u32[]{:S(2)}, u32[]{:S(2)}) %collective-permute-start.6) | collective-permute-done | bytes 1310752 | tf_op jit(solution)/shard_map/ppermute | solution.py:28
  142.7 5.9 collective-permute-start.9
  150.7 20.2 %collective-permute-done.8 = f32[4,40,2048]{2,1,0:T(8,128)S(1)} collective-permute-done((f32[4,40,2048]{2,1,0:T(8,128)S(1)}, f32[4,40,2048]{2,1,0:T(8,128)S(1)}, u32[]{:S(2)}, u32[]{:S(2)}) %collective-permute-start.8) | collective-permute-done | bytes 1310752 | tf_op jit(solution)/shard_map/ppermute | solution.py:17
  177.5 6.5 %collective-permute-start.11 = (f32[4,40,2048]{2,1,0:T(8,128)S(1)}, f32[4,40,2048]{2,1,0:T(8,128)S(1)}, u32[]{:S(2)}, u32[]{:S(2)}) collective-permute-start(f32[4,40,2048]{2,1,0:T(8,128)S(1)} %get-tuple-element.10), channel_id=1, source_target_pairs={{1,0},{2,1},{3,2},{4,3},{5,4},{6,5},{7,6},{8,7},{9,8},{10,9},{11,1... | collective-permute-start | bytes 3932168 | tf_op jit(solution)/shard_map/ppermute | solution.py:30
  184.0 23.1 %collective-permute-done.10 = f32[4,40,2048]{2,1,0:T(8,128)S(1)} collective-permute-done((f32[4,40,2048]{2,1,0:T(8,128)S(1)}, f32[4,40,2048]{2,1,0:T(8,128)S(1)}, u32[]{:S(2)}, u32[]{:S(2)}) %collective-permute-start.10) | collective-permute-done | bytes 1310752 | tf_op jit(solution)/shard_map/ppermute | solution.py:28
  216.5 7.0 %collective-permute-start.13 = (f32[4,40,2048]{2,1,0:T(8,128)S(1)}, f32[4,40,2048]{2,1,0:T(8,128)S(1)}, u32[]{:S(2)}, u32[]{:S(2)}) collective-permute-start(f32[4,40,2048]{2,1,0:T(8,128)S(1)} %convolution_bitcast_fusion.2), channel_id=1, source_target_pairs={{1,0},{2,1},{3,2},{4,3},{5,4},{6,5},{7,6},{8,7},{9,8},{10,9},{11,1... | collective-permute-start | bytes 3932168 | tf_op jit(solution)/shard_map/ppermute | solution.py:17
  225.5 18.1 %collective-permute-done.12 = f32[4,40,2048]{2,1,0:T(8,128)S(1)} collective-permute-done((f32[4,40,2048]{2,1,0:T(8,128)S(1)}, f32[4,40,2048]{2,1,0:T(8,128)S(1)}, u32[]{:S(2)}, u32[]{:S(2)}) %collective-permute-start.12) | collective-permute-done | bytes 1310752 | tf_op jit(solution)/shard_map/ppermute | solution.py:17
  250.3 6.5 %collective-permute-start.15 = (f32[4,40,2048]{2,1,0:T(8,128)S(1)}, f32[4,40,2048]{2,1,0:T(8,128)S(1)}, u32[]{:S(2)}, u32[]{:S(2)}) collective-permute-start(f32[4,40,2048]{2,1,0:T(8,128)S(1)} %get-tuple-element.8), channel_id=1, source_target_pairs={{1,0},{2,1},{3,2},{4,3},{5,4},{6,5},{7,6},{8,7},{9,8},{10,9},{11,1... | collective-permute-start | bytes 3932168 | tf_op jit(solution)/shard_map/ppermute | solution.py:30
  256.9 21.3 %collective-permute-done.14 = f32[4,40,2048]{2,1,0:T(8,128)S(1)} collective-permute-done((f32[4,40,2048]{2,1,0:T(8,128)S(1)}, f32[4,40,2048]{2,1,0:T(8,128)S(1)}, u32[]{:S(2)}, u32[]{:S(2)}) %collective-permute-start.14) | collective-permute-done | bytes 1310752 | tf_op jit(solution)/shard_map/ppermute | solution.py:28
  287.5 6.7 %collective-permute-start.17 = (f32[4,40,2048]{2,1,0:T(8,128)S(1)}, f32[4,40,2048]{2,1,0:T(8,128)S(1)}, u32[]{:S(2)}, u32[]{:S(2)}) collective-permute-start(f32[4,40,2048]{2,1,0:T(8,128)S(1)} %convolution_bitcast_fusion), channel_id=1, source_target_pairs={{1,0},{2,1},{3,2},{4,3},{5,4},{6,5},{7,6},{8,7},{9,8},{10,9},{11,1... | collective-permute-start | bytes 3932168 | tf_op jit(solution)/shard_map/ppermute | solution.py:17
  296.2 16.5 %collective-permute-done.16 = f32[4,40,2048]{2,1,0:T(8,128)S(1)} collective-permute-done((f32[4,40,2048]{2,1,0:T(8,128)S(1)}, f32[4,40,2048]{2,1,0:T(8,128)S(1)}, u32[]{:S(2)}, u32[]{:S(2)}) %collective-permute-start.16) | collective-permute-done | bytes 1310752 | tf_op jit(solution)/shard_map/ppermute | solution.py:17
  322.8 6.3 %copy.21 = f32[64,32,720]{2,1,0:T(8,128)} copy(f32[64,32,720]{2,0,1:T(8,128)S(1)} %fusion.67) | data formatting | bytes 11796480 | tf_op jit(solution)/shard_map/kb,bqc->kqc/dot_general | solution.py:107
  329.2 224.3 %reduce-scatter.2.cloned.1.call-done = f32[64,720]{1,0:T(8,128)} async-done(((f32[2048,720]{1,0:T(8,128)}), f32[64,720]{1,0:T(8,128)}) %reduce-scatter.2.cloned.1.call-update) | async-done | bytes 184336 | tf_op jit(solution)/shard_map/reduce_scatter | solution.py:106
  553.5 28.1 %all-gather.3.cloned.1.call-done = f32[512,720]{1,0:T(8,128)} async-done(((f32[64,720]{1,0:T(8,128)}), f32[512,720]{1,0:T(8,128)}) %all-gather.3.cloned.1.call-update) | async-done | bytes 1474576 | tf_op jit(solution)/shard_map/all_gather | solution.py:112
  (73 shorter events, 77.8 us)
Async XLA Ops:
  6.5 312.5 %copy-start = (bf16[1,2048,720]{1,2,0:T(8,128)(2,1)S(1)}, bf16[1,2048,720]{1,2,0:T(8,128)(2,1)}, u32[]{:S(2)}) copy-start(bf16[1,2048,720]{1,2,0:T(8,128)(2,1)} %param.11) | copy-start | bytes 8847364
  6.5 13.3 %copy-start.5 = (s32[64]{0:T(128)S(1)}, s32[64]{0:T(128)}, u32[]{:S(2)}) copy-start(s32[64]{0:T(128)} %param.8) | copy-start | bytes 772
  6.5 13.4 %copy-start.3 = (f32[64,65]{1,0:T(8,128)S(1)}, f32[64,65]{1,0:T(8,128)}, u32[]{:S(2)}) copy-start(f32[64,65]{1,0:T(8,128)} %param.7) | copy-start | bytes 49924
  6.5 546.9 %reduce-scatter.2.cloned.1.call-start = ((), (), s32[]{:S(2)}) async-start(), calls=%async_computation.1 | async-start | bytes 6488064 | tf_op jit(solution)/shard_map/reduce_scatter | solution.py:106
  10.2 36.7 %collective-permute-start = (f32[4,40,2048]{2,1,0:T(8,128)}, f32[4,40,2048]{2,1,0:T(8,128)}, u32[]{:S(2)}, u32[]{:S(2)}) collective-permute-start(f32[4,40,2048]{2,1,0:T(8,128)} %get-tuple-element.13), channel_id=1, source_target_pairs={{0,1},{1,2},{2,3},{3,4},{4,5},{5,6},{6,7},{7,8},{8,9},{9,10},{10,1... | collective-permute-start | bytes 3932168 | tf_op jit(solution)/shard_map/ppermute | solution.py:28
  14.0 34.1 %collective-permute-start.1 = (f32[4,40,2048]{2,1,0:T(8,128)}, f32[4,40,2048]{2,1,0:T(8,128)}, u32[]{:S(2)}, u32[]{:S(2)}) collective-permute-start(f32[4,40,2048]{2,1,0:T(8,128)} %get-tuple-element.14), channel_id=1, source_target_pairs={{1,0},{2,1},{3,2},{4,3},{5,4},{6,5},{7,6},{8,7},{9,8},{10,9},{11,1... | collective-permute-start | bytes 3932168 | tf_op jit(solution)/shard_map/ppermute | solution.py:30
  55.9 39.6 %collective-permute-start.2 = (f32[4,40,2048]{2,1,0:T(8,128)S(1)}, f32[4,40,2048]{2,1,0:T(8,128)S(1)}, u32[]{:S(2)}, u32[]{:S(2)}) collective-permute-start(f32[4,40,2048]{2,1,0:T(8,128)S(1)} %convolution_bitcast_fusion.7), channel_id=1, source_target_pairs={{0,1},{1,2},{2,3},{3,4},{4,5},{5,6},{6,7},{7,8},{8,9},{9,10},{10,1... | collective-permute-start | bytes 3932168 | tf_op jit(solution)/shard_map/ppermute | solution.py:17
  59.8 37.0 %collective-permute-start.3 = (f32[4,40,2048]{2,1,0:T(8,128)S(1)}, f32[4,40,2048]{2,1,0:T(8,128)S(1)}, u32[]{:S(2)}, u32[]{:S(2)}) collective-permute-start(f32[4,40,2048]{2,1,0:T(8,128)S(1)} %convolution_bitcast_fusion.6), channel_id=1, source_target_pairs={{1,0},{2,1},{3,2},{4,3},{5,4},{6,5},{7,6},{8,7},{9,8},{10,9},{11,1... | collective-permute-start | bytes 3932168 | tf_op jit(solution)/shard_map/ppermute | solution.py:17
  66.0 27.1 %collective-permute-start.5 = (f32[1,40,1]{1,2,0:T(1,128)S(1)}, f32[1,40,1]{1,2,0:T(1,128)S(1)}, u32[]{:S(2)}, u32[]{:S(2)}) collective-permute-start(f32[1,40,1]{1,2,0:T(1,128)S(1)} %bitcast.194), channel_id=1, source_target_pairs={{1,0},{2,1},{3,2},{4,3},{5,4},{6,5},{7,6},{8,7},{9,8},{10,9},{11,1... | collective-permute-start | bytes 488 | tf_op jit(solution)/shard_map/ppermute | solution.py:17
  69.9 23.3 %collective-permute-start.4 = (f32[1,40,1]{1,2,0:T(1,128)S(1)}, f32[1,40,1]{1,2,0:T(1,128)S(1)}, u32[]{:S(2)}, u32[]{:S(2)}) collective-permute-start(f32[1,40,1]{1,2,0:T(1,128)S(1)} %bitcast.193), channel_id=1, source_target_pairs={{0,1},{1,2},{2,3},{3,4},{4,5},{5,6},{6,7},{7,8},{8,9},{9,10},{10,1... | collective-permute-start | bytes 488 | tf_op jit(solution)/shard_map/ppermute | solution.py:17
  99.1 33.4 %collective-permute-start.6 = (f32[4,40,2048]{2,1,0:T(8,128)S(1)}, f32[4,40,2048]{2,1,0:T(8,128)S(1)}, u32[]{:S(2)}, u32[]{:S(2)}) collective-permute-start(f32[4,40,2048]{2,1,0:T(8,128)S(1)} %get-tuple-element.11), channel_id=1, source_target_pairs={{0,1},{1,2},{2,3},{3,4},{4,5},{5,6},{6,7},{7,8},{8,9},{9,10},{10,1... | collective-permute-start | bytes 3932168 | tf_op jit(solution)/shard_map/ppermute | solution.py:28
  103.1 30.6 %collective-permute-start.7 = (f32[4,40,2048]{2,1,0:T(8,128)S(1)}, f32[4,40,2048]{2,1,0:T(8,128)S(1)}, u32[]{:S(2)}, u32[]{:S(2)}) collective-permute-start(f32[4,40,2048]{2,1,0:T(8,128)S(1)} %get-tuple-element.12), channel_id=1, source_target_pairs={{1,0},{2,1},{3,2},{4,3},{5,4},{6,5},{7,6},{8,7},{9,8},{10,9},{11,1... | collective-permute-start | bytes 3932168 | tf_op jit(solution)/shard_map/ppermute | solution.py:30
  138.4 32.5 %collective-permute-start.8 = (f32[4,40,2048]{2,1,0:T(8,128)S(1)}, f32[4,40,2048]{2,1,0:T(8,128)S(1)}, u32[]{:S(2)}, u32[]{:S(2)}) collective-permute-start(f32[4,40,2048]{2,1,0:T(8,128)S(1)} %convolution_bitcast_fusion.5), channel_id=1, source_target_pairs={{0,1},{1,2},{2,3},{3,4},{4,5},{5,6},{6,7},{7,8},{8,9},{9,10},{10,1... | collective-permute-start | bytes 3932168 | tf_op jit(solution)/shard_map/ppermute | solution.py:17
  142.7 30.9 %collective-permute-start.9 = (f32[4,40,2048]{2,1,0:T(8,128)S(1)}, f32[4,40,2048]{2,1,0:T(8,128)S(1)}, u32[]{:S(2)}, u32[]{:S(2)}) collective-permute-start(f32[4,40,2048]{2,1,0:T(8,128)S(1)} %convolution_bitcast_fusion.4), channel_id=1, source_target_pairs={{1,0},{2,1},{3,2},{4,3},{5,4},{6,5},{7,6},{8,7},{9,8},{10,9},{11,1... | collective-permute-start | bytes 3932168 | tf_op jit(solution)/shard_map/ppermute | solution.py:17
  175.6 31.6 %collective-permute-start.10 = (f32[4,40,2048]{2,1,0:T(8,128)S(1)}, f32[4,40,2048]{2,1,0:T(8,128)S(1)}, u32[]{:S(2)}, u32[]{:S(2)}) collective-permute-start(f32[4,40,2048]{2,1,0:T(8,128)S(1)} %get-tuple-element.9), channel_id=1, source_target_pairs={{0,1},{1,2},{2,3},{3,4},{4,5},{5,6},{6,7},{7,8},{8,9},{9,10},{10,1... | collective-permute-start | bytes 3932168 | tf_op jit(solution)/shard_map/ppermute | solution.py:28
  177.5 30.8 %collective-permute-start.11 = (f32[4,40,2048]{2,1,0:T(8,128)S(1)}, f32[4,40,2048]{2,1,0:T(8,128)S(1)}, u32[]{:S(2)}, u32[]{:S(2)}) collective-permute-start(f32[4,40,2048]{2,1,0:T(8,128)S(1)} %get-tuple-element.10), channel_id=1, source_target_pairs={{1,0},{2,1},{3,2},{4,3},{5,4},{6,5},{7,6},{8,7},{9,8},{10,9},{11,1... | collective-permute-start | bytes 3932168 | tf_op jit(solution)/shard_map/ppermute | solution.py:30
  213.0 30.6 %collective-permute-start.12 = (f32[4,40,2048]{2,1,0:T(8,128)S(1)}, f32[4,40,2048]{2,1,0:T(8,128)S(1)}, u32[]{:S(2)}, u32[]{:S(2)}) collective-permute-start(f32[4,40,2048]{2,1,0:T(8,128)S(1)} %convolution_bitcast_fusion.3), channel_id=1, source_target_pairs={{0,1},{1,2},{2,3},{3,4},{4,5},{5,6},{6,7},{7,8},{8,9},{9,10},{10,1... | collective-permute-start | bytes 3932168 | tf_op jit(solution)/shard_map/ppermute | solution.py:17
  216.5 29.9 %collective-permute-start.13 = (f32[4,40,2048]{2,1,0:T(8,128)S(1)}, f32[4,40,2048]{2,1,0:T(8,128)S(1)}, u32[]{:S(2)}, u32[]{:S(2)}) collective-permute-start(f32[4,40,2048]{2,1,0:T(8,128)S(1)} %convolution_bitcast_fusion.2), channel_id=1, source_target_pairs={{1,0},{2,1},{3,2},{4,3},{5,4},{6,5},{7,6},{8,7},{9,8},{10,9},{11,1... | collective-permute-start | bytes 3932168 | tf_op jit(solution)/shard_map/ppermute | solution.py:17
  248.4 29.7 %collective-permute-start.14 = (f32[4,40,2048]{2,1,0:T(8,128)S(1)}, f32[4,40,2048]{2,1,0:T(8,128)S(1)}, u32[]{:S(2)}, u32[]{:S(2)}) collective-permute-start(f32[4,40,2048]{2,1,0:T(8,128)S(1)} %get-tuple-element.7), channel_id=1, source_target_pairs={{0,1},{1,2},{2,3},{3,4},{4,5},{5,6},{6,7},{7,8},{8,9},{9,10},{10,1... | collective-permute-start | bytes 3932168 | tf_op jit(solution)/shard_map/ppermute | solution.py:28
  250.3 29.0 %collective-permute-start.15 = (f32[4,40,2048]{2,1,0:T(8,128)S(1)}, f32[4,40,2048]{2,1,0:T(8,128)S(1)}, u32[]{:S(2)}, u32[]{:S(2)}) collective-permute-start(f32[4,40,2048]{2,1,0:T(8,128)S(1)} %get-tuple-element.8), channel_id=1, source_target_pairs={{1,0},{2,1},{3,2},{4,3},{5,4},{6,5},{7,6},{8,7},{9,8},{10,9},{11,1... | collective-permute-start | bytes 3932168 | tf_op jit(solution)/shard_map/ppermute | solution.py:30
  284.0 28.8 %collective-permute-start.16 = (f32[4,40,2048]{2,1,0:T(8,128)S(1)}, f32[4,40,2048]{2,1,0:T(8,128)S(1)}, u32[]{:S(2)}, u32[]{:S(2)}) collective-permute-start(f32[4,40,2048]{2,1,0:T(8,128)S(1)} %convolution_bitcast_fusion.1), channel_id=1, source_target_pairs={{0,1},{1,2},{2,3},{3,4},{4,5},{5,6},{6,7},{7,8},{8,9},{9,10},{10,1... | collective-permute-start | bytes 3932168 | tf_op jit(solution)/shard_map/ppermute | solution.py:17
  287.5 28.0 %collective-permute-start.17 = (f32[4,40,2048]{2,1,0:T(8,128)S(1)}, f32[4,40,2048]{2,1,0:T(8,128)S(1)}, u32[]{:S(2)}, u32[]{:S(2)}) collective-permute-start(f32[4,40,2048]{2,1,0:T(8,128)S(1)} %convolution_bitcast_fusion), channel_id=1, source_target_pairs={{1,0},{2,1},{3,2},{4,3},{5,4},{6,5},{7,6},{8,7},{9,8},{10,9},{11,1... | collective-permute-start | bytes 3932168 | tf_op jit(solution)/shard_map/ppermute | solution.py:17
  314.0 3.1 copy-start.2
  329.1 252.5 %all-gather.3.cloned.1.call-start = ((), (), s32[]{:S(2)}) async-start(), calls=%async_computation.2 | async-start | bytes 1769472 | tf_op jit(solution)/shard_map/all_gather | solution.py:112
  (2 other events, 2.6 us)
Sparse Core Ops, SparseCore 0:
  329.2 224.2 reduce-scatter.1
  555.5 26.1 all-gather.2
